TPU v7x, 256 devices: a whole 4x4x8 slice. The times are simulated.
256 devices in a mesh: dp: 32 (over z, x_hi, core), fsdp: 8 (over x_lo, y).
Axes of the slice: x: 4 (x_hi: 2, x_lo: 2; x = x_hi * 2 + x_lo), y: 4, z: 8, core: 2. Of those that a mesh axis runs over, the one named last changes fastest.
Arguments:
- query_rows: bfloat16 [32768, 2048], P(('dp', 'fsdp')), may hold values from -12 to 12
- key_rows: bfloat16 [32768, 2048], P(('dp', 'fsdp')), may hold values from -12 to 12
- value_rows: bfloat16 [32768, 2048], P(('dp', 'fsdp')), may hold values from -6 to 6
- out_grad: bfloat16 [32768, 2048], P(('dp', 'fsdp')), may hold values from -6 to 6
- params: float32 [65536, 2048], P(('dp', 'fsdp')), may hold values from -6 to 6
- momentum: float32 [65536, 2048], P(('dp', 'fsdp')), may hold values from -3 to 3
- token_ids: int32 [32768], P(('dp', 'fsdp')), may hold values from 0 to 8191
- block_mask: int32 [8, 8], replicated, may hold values from 0 to 1, as said below
- step_index: int32 [1], replicated, may hold values from 0 to 7
Outputs:
- grad_query: bfloat16 [32768, 2048], P(('dp', 'fsdp'))
- grad_key: bfloat16 [32768, 2048], P(('dp', 'fsdp'))
- grad_value: bfloat16 [32768, 2048], P(('dp', 'fsdp'))
- new_params: float32 [65536, 2048], P(('dp', 'fsdp'))
- new_momentum: float32 [65536, 2048], P(('dp', 'fsdp'))
Inputs may be any that keep to these rules, and one draw needn't show every extreme that they name: block_mask[i, i] is 1 and block_mask[i, j] is 0 for j > i.
All inputs are finite; a program needn't handle non-finite values.
Results may differ from a plain program's by a relative error of at most 0.0095.
Values may be sent and summed in bfloat16 or wider, within the bound.
A program may use at most 128 MiB of HBM per device.

v0:
```python
import math

import jax
import jax.numpy as jnp
from jax import lax
from jax.sharding import PartitionSpec as P

HD = 128
CODES = 2048
INNER = 2048


MOMENTUM_RATE = 0.9
LEARN_RATE = 0.25


def as_sent(value):

    def short(part):
        return part.astype(jnp.bfloat16) if part.dtype == jnp.float32 else part

    return jax.tree.map(short, value)


def swapped(block, axis, distance):
    count = lax.axis_size(axis)
    route = []
    for low in range(count):
        high = low | 1 << distance
        if high != low and high < count:
            route += [(low, high), (high, low)]
    return lax.ppermute(block, axis, route)


def head_attention(query_rows, key_rows, value_rows, grad_rows, stem_ids, block_mask):
    tokens = query_rows.shape[0]
    local_heads = query_rows.shape[1] // HD
    blocks = block_mask.shape[0]
    block_rows = tokens // blocks
    score_scale = 1.0 / math.sqrt(HD)
    query_h = query_rows.reshape(tokens, local_heads, HD)
    key_h = key_rows.reshape(tokens, local_heads, HD)
    value_h = value_rows.reshape(tokens, local_heads, HD)
    grad_h = grad_rows.reshape(tokens, local_heads, HD)
    spread = jnp.broadcast_to(
        block_mask[:, None, :, None], (blocks, block_rows, blocks, block_rows)
    ).reshape(tokens, tokens)
    position = jnp.arange(tokens, dtype=jnp.int32)
    block_of = position // block_rows
    allowed = (
        (spread == 1)
        & (position[None, :] <= position[:, None])
        & ((stem_ids[:, None] == stem_ids[None, :]) | (block_of[:, None] == block_of[None, :]))
    )
    scores = (
        jnp.einsum("qhd,khd->hqk", query_h, key_h, preferred_element_type=jnp.float32) * score_scale
    )
    scores = jnp.where(allowed[None], scores, -1e30)
    top_score = jnp.max(scores, axis=-1, keepdims=True)
    exp_terms = jnp.where(allowed[None], jnp.exp(scores - top_score), 0.0)
    prob_f32 = exp_terms / jnp.sum(exp_terms, axis=-1, keepdims=True)
    prob_b16 = prob_f32.astype(jnp.bfloat16)
    attended = jnp.einsum(
        "hqk,khd->qhd", prob_b16, value_h, preferred_element_type=jnp.float32
    ).astype(jnp.bfloat16)
    grad_value = jnp.einsum(
        "hqk,qhd->khd", prob_b16, grad_h, preferred_element_type=jnp.float32
    ).astype(jnp.bfloat16)
    grad_prob = jnp.einsum("qhd,khd->hqk", grad_h, value_h, preferred_element_type=jnp.float32)
    row_dot = jnp.sum(prob_f32 * grad_prob, axis=-1, keepdims=True)
    grad_score = (prob_f32 * (grad_prob - row_dot) * score_scale).astype(jnp.bfloat16)
    grad_query = jnp.einsum(
        "hqk,khd->qhd", grad_score, key_h, preferred_element_type=jnp.float32
    ).astype(jnp.bfloat16)
    grad_key = jnp.einsum(
        "hqk,qhd->khd", grad_score, query_h, preferred_element_type=jnp.float32
    ).astype(jnp.bfloat16)
    flat_shape = (tokens, local_heads * HD)
    return (
        attended.reshape(flat_shape),
        grad_query.reshape(flat_shape),
        grad_key.reshape(flat_shape),
        grad_value.reshape(flat_shape),
    )


def swap_updated(carried, shift_bit):

    def branch(bit_level):

        def moved(payload):
            return jax.tree.map(
                lambda part, own: part.astype(own.dtype),
                swapped(as_sent(payload), "dp", bit_level),
                payload,
            )

        return moved

    return lax.switch(shift_bit, [branch(bit_level) for bit_level in range(4)], carried)


def shards(
    query_rows, key_rows, value_rows, out_grad, params, momentum, token_ids, block_mask, step_index
):
    inv_width = 1.0 / math.sqrt(INNER)
    step_value = step_index[0]
    shift_bit = step_value % 4
    correction = 1.0 / (
        1.0 - jnp.exp((step_value + 1).astype(jnp.float32) * math.log(MOMENTUM_RATE))
    )
    weight16 = params.astype(jnp.bfloat16)
    stem_ids = lax.all_gather(token_ids, "fsdp", axis=0, tiled=True) // CODES
    grad_tok = (
        lax.dot_general(
            out_grad,
            lax.all_gather(weight16, "fsdp", axis=0, tiled=True),
            (((1,), (1,)), ((), ())),
            preferred_element_type=jnp.float32,
        )
        * inv_width
    ).astype(jnp.bfloat16)
    grad_rows = lax.all_to_all(grad_tok, "fsdp", split_axis=1, concat_axis=0, tiled=True)
    query_h, key_h, value_h = (
        lax.all_to_all(query_rows, "fsdp", split_axis=1, concat_axis=0, tiled=True),
        lax.all_to_all(key_rows, "fsdp", split_axis=1, concat_axis=0, tiled=True),
        lax.all_to_all(value_rows, "fsdp", split_axis=1, concat_axis=0, tiled=True),
    )
    attended, grad_query, grad_key, grad_value = head_attention(
        query_h, key_h, value_h, grad_rows, stem_ids, block_mask
    )
    attended_tok, query_grad, key_grad, value_grad = (
        lax.all_to_all(attended, "fsdp", split_axis=0, concat_axis=1, tiled=True),
        lax.all_to_all(grad_query, "fsdp", split_axis=0, concat_axis=1, tiled=True),
        lax.all_to_all(grad_key, "fsdp", split_axis=0, concat_axis=1, tiled=True),
        lax.all_to_all(grad_value, "fsdp", split_axis=0, concat_axis=1, tiled=True),
    )
    grad_weight = (
        lax.psum_scatter(
            lax.dot_general(
                attended_tok, out_grad, (((0,), (0,)), ((), ())), preferred_element_type=jnp.float32
            ).astype(jnp.bfloat16),
            "fsdp",
            scatter_dimension=0,
            tiled=True,
        ).astype(jnp.float32)
        * inv_width
    )
    moment = MOMENTUM_RATE * momentum + grad_weight
    stepped = params - LEARN_RATE * correction * moment
    other_stepped, other_moment = swap_updated((stepped, moment), shift_bit)
    new_params = 0.5 * (stepped + other_stepped)
    new_momentum = 0.5 * (moment + other_moment)
    return (query_grad, key_grad, value_grad, new_params, new_momentum)


def solution(mesh):
    placed = (
        P(("dp", "fsdp"), None),
        P(("dp", "fsdp"), None),
        P(("dp", "fsdp"), None),
        P(("dp", "fsdp"), None),
        P(("dp", "fsdp"), None),
        P(("dp", "fsdp"), None),
        P(("dp", "fsdp")),
        P(),
        P(),
    )
    return jax.shard_map(
        shards,
        mesh=mesh,
        in_specs=placed,
        out_specs=(
            P(("dp", "fsdp"), None),
            P(("dp", "fsdp"), None),
            P(("dp", "fsdp"), None),
            P(("dp", "fsdp"), None),
            P(("dp", "fsdp"), None),
        ),
        check_vma=False,
    )
```

profile of v0, /device:TPU:2, one launch (start us, length us, event | category | flops | bytes accessed | tf_op | source)
XLA Modules:
  0.0 433.4 jit_solution(233387828773668622)
XLA Ops:
  7.2 2.1 copy.65
  9.3 5.9 %all-to-all-start = ((bf16[128,8,256]{0,2,1:T(8,128)(2,1)}), bf16[128,8,256]{0,2,1:T(8,128)(2,1)S(1)}, u32[]{:S(2)}, u32[]{:S(2)}) async-start(bf16[128,8,256]{0,2,1:T(8,128)(2,1)} %bitcast.2), calls=%async_computation | async-start | bytes 1048576 | tf_op jit(solution)/shard_map/all_to_all | solution.py:125
  15.2 2.0 copy.67
  17.3 6.6 %all-to-all-done = bf16[128,8,256]{0,2,1:T(8,128)(2,1)S(1)} async-done(((bf16[128,8,256]{0,2,1:T(8,128)(2,1)}), bf16[128,8,256]{0,2,1:T(8,128)(2,1)S(1)}, u32[]{:S(2)}, u32[]{:S(2)}) %all-to-all-start) | async-done | bytes 524320 | tf_op jit(solution)/shard_map/all_to_all | solution.py:125
  23.8 4.3 all-to-all-start.1
  28.9 2.0 copy.73
  31.0 17.9 %all-gather = s32[8,1,128]{2,1,0:T(1,128)S(1)} all-gather(s32[1,1,128]{2,1,0:T(1,128)} %bitcast.99), channel_id=1, replica_groups=mesh['dp'=32,'fsdp'=8] {'fsdp'}, dimensions={0}, use_global_device_ids=true | all-gather | bytes 4608 | tf_op jit(solution)/shard_map/all_gather | solution.py:113
  48.9 4.9 %all-to-all-start.3 = ((bf16[128,8,256]{0,2,1:T(8,128)(2,1)}), bf16[128,8,256]{0,2,1:T(8,128)(2,1)S(1)}, u32[]{:S(2)}, u32[]{:S(2)}) async-start(bf16[128,8,256]{0,2,1:T(8,128)(2,1)} %bitcast.8), calls=%async_computation.3 | async-start | bytes 1048576 | tf_op jit(solution)/shard_map/all_to_all | solution.py:127
  54.2 2.5 fusion.9
  57.9 3.2 all-to-all-done.3
  61.7 7.8 %fusion.56 = (f32[2,1024]{1,0:T(2,128)S(1)}, f32[2,1024,1024]{1,2,0:T(8,128)}) fusion(pred[1024,1024]{0,1:T(8,128)(4,1)} %fusion.9, bf16[1024,2,128]{0,2,1:T(8,128)(2,1)S(1)} %reshape.165, bf16[1024,2,128]{0,2,1:T(8,128)(2,1)S(1)} %reshape.166), kind=kOutput, calls=%fused_computation.57 | convolution fusion | flops 547357696 | bytes 10493952 | tf_op jit(solution)/shard_map/sub | solution.py:60
  69.5 5.1 %fusion.40 = bf16[1024,2,128]{2,0,1:T(8,128)(2,1)S(1)} fusion(bf16[1024,2,128]{0,2,1:T(8,128)(2,1)S(1)} %reshape.168, f32[2,1024,1024]{1,2,0:T(8,128)} %get-tuple-element.65, f32[2,1024]{1,0:T(2,128)S(1)} %get-tuple-element.64), kind=kOutput, calls=%fused_computation.34 | convolution fusion | flops 541327360 | bytes 9445376 | tf_op jit(solution)/shard_map/hqk,khd->qhd/dot_general | solution.py:63
  75.0 11.2 %all_to_all.140 = bf16[8,128,256]{1,2,0:T(8,128)(2,1)S(1)} all-to-all(bf16[8,128,256]{1,2,0:T(8,128)(2,1)S(1)} %copy.89), channel_id=1, replica_groups=mesh['dp'=32,'fsdp'=8] {'fsdp'}, dimensions={0} | all-to-all | bytes 1048576 | tf_op jit(solution)/shard_map/all_to_all | solution.py:133
  86.2 5.6 %convolution_convert_fusion = bf16[2048,2048]{1,0:T(8,128)(2,1)} fusion(bf16[128,2048]{0,1:T(8,128)(2,1)S(1)} %bitcast.83, bf16[128,2048]{1,0:T(8,128)(2,1)S(1)} %copy-done), kind=kOutput, calls=%fused_computation.7 | convolution fusion | flops 1077936128 | bytes 9437184 | tf_op jit(solution)/shard_map/dot_general | solution.py:140
  92.7 94.8 %reduce-scatter.2.cloned.1.call-done = bf16[256,2048]{1,0:T(8,128)(2,1)} async-done(((bf16[2048,2048]{1,0:T(8,128)(2,1)}), bf16[256,2048]{1,0:T(8,128)(2,1)}) %reduce-scatter.2.cloned.1.call-update) | async-done | bytes 1048592 | tf_op jit(solution)/shard_map/reduce_scatter | solution.py:139
  187.5 5.9 %multiply_subtract_fusion = (f32[256,2048]{1,0:T(8,128)S(1)}, f32[256,2048]{1,0:T(8,128)}, bf16[256,2048]{1,0:T(8,128)(2,1)}) fusion(f32[256,2048]{1,0:T(8,128)} %param.17, f32[]{:T(128)S(6)} %mul_shard_map.3, bf16[256,2048]{1,0:T(8,128)(2,1)} %reduce-scatter.2.cloned.1.call-done, f32[256,2048]{1,0:T(8,128)} %param.18), kind=kLoop, calls=%fused_computation.22 | loop fusion | flops 3670016 | bytes 10485764 | tf_op jit(solution)/shard_map/sub | solution.py:150
  193.4 93.4 %all-gather.3.cloned.1.call-done = bf16[2048,2048]{1,0:T(8,128)(2,1)} async-done(((bf16[256,2048]{1,0:T(8,128)(2,1)}), bf16[2048,2048]{1,0:T(8,128)(2,1)}) %all-gather.3.cloned.1.call-update) | async-done | bytes 8388624 | tf_op jit(solution)/shard_map/all_gather | solution.py:117
  286.9 7.1 %fusion.17 = bf16[128,2048]{1,0:T(8,128)(2,1)} fusion(bf16[128,2048]{1,0:T(8,128)(2,1)S(1)} %copy-done, bf16[2048,2048]{1,0:T(8,128)(2,1)} %all-gather.3.cloned.1.call-done), kind=kOutput, calls=%fused_computation.19 | convolution fusion | flops 1074266112 | bytes 9437184 | tf_op jit(solution)/shard_map/dot_general | solution.py:115
  295.2 12.6 %all_to_all.141 = bf16[128,8,256]{0,2,1:T(8,128)(2,1)S(1)} all-to-all(bf16[128,8,256]{0,2,1:T(8,128)(2,1)S(1)} %bitcast.90), channel_id=1, replica_groups=mesh['dp'=32,'fsdp'=8] {'fsdp'}, dimensions={1} | all-to-all | bytes 1048576 | tf_op jit(solution)/shard_map/all_to_all | solution.py:123
  310.3 4.9 %fusion.22 = bf16[2,128,1024]{2,1,0:T(8,128)(2,1)S(1)} fusion(bf16[1024,2,128]{0,2,1:T(8,128)(2,1)S(1)} %reshape.167, f32[2,1024,1024]{1,2,0:T(8,128)} %get-tuple-element.65, f32[2,1024]{1,0:T(2,128)S(1)} %get-tuple-element.64), kind=kOutput, calls=%fused_computation.28 | convolution fusion | flops 541327360 | bytes 9445376 | tf_op jit(solution)/shard_map/hqk,qhd->khd/dot_general | solution.py:66
  316.2 5.5 %all-to-all-start.6 = ((bf16[8,128,256]{1,2,0:T(8,128)(2,1)}), bf16[8,128,256]{1,2,0:T(8,128)(2,1)}, u32[]{:S(2)}, u32[]{:S(2)}) async-start(bf16[8,128,256]{1,2,0:T(8,128)(2,1)} %copy.85), calls=%async_computation.6 | async-start | bytes 1048576 | tf_op jit(solution)/shard_map/all_to_all | solution.py:136
  321.6 4.5 %fusion.57 = f32[2,1024,1024]{1,2,0:T(8,128)} fusion(bf16[1024,2,128]{0,2,1:T(8,128)(2,1)S(1)} %reshape.167, bf16[1024,2,128]{0,2,1:T(8,128)(2,1)S(1)} %reshape.168), kind=kOutput, calls=%fused_computation.58 | convolution fusion | flops 536870912 | bytes 9437184 | tf_op jit(solution)/shard_map/qhd,khd->hqk/dot_general | solution.py:69
  326.2 12.8 %fusion.37 = bf16[1024,2,128]{2,0,1:T(8,128)(2,1)S(1)} fusion(bf16[1024,2,128]{0,2,1:T(8,128)(2,1)} %copy-done.4, f32[2,1024,1024]{1,2,0:T(8,128)} %fusion.57, f32[2,1024,1024]{1,2,0:T(8,128)} %get-tuple-element.65, f32[2,1024]{1,0:T(2,128)S(1)} %get-tuple-element.64), kind=kOutput, calls=%fused_computation.33 | convolution fusion | flops 551816192 | bytes 17833984 | tf_op jit(solution)/shard_map/hqk,khd->qhd/dot_general | solution.py:72
  340.2 5.7 %all-to-all-start.4 = ((bf16[8,128,256]{1,2,0:T(8,128)(2,1)}), bf16[8,128,256]{1,2,0:T(8,128)(2,1)S(1)}, u32[]{:S(2)}, u32[]{:S(2)}) async-start(bf16[8,128,256]{1,2,0:T(8,128)(2,1)} %copy.80), calls=%async_computation.4 | async-start | bytes 1048576 | tf_op jit(solution)/shard_map/all_to_all | solution.py:134
  345.9 48.3 %conditional.4 = (f32[256,2048]{1,0:T(8,128)}, f32[256,2048]{1,0:T(8,128)}) conditional(s32[]{:T(128)} %clamp.3, (f32[256,2048]{1,0:T(8,128)S(1)}, f32[256,2048]{1,0:T(8,128)}) %tuple.50, (f32[256,2048]{1,0:T(8,128)S(1)}, f32[256,2048]{1,0:T(8,128)}) %tuple.50, (f32[256,2048]{1,0:T(8,128)S(1)}, ...), branch_computations={%region_4.5_spmd, %region_5.6_spmd, %region_6.7_spmd, %region_7.8_... | conditional | flops 2097152 | bytes 20971616
  350.1 23.8 %collective-permute-done.5 = bf16[256,2048]{1,0:T(8,128)(2,1)S(1)} collective-permute-done((bf16[256,2048]{1,0:T(8,128)(2,1)S(1)}, bf16[256,2048]{1,0:T(8,128)(2,1)S(1)}, u32[]{:S(2)}, u32[]{:S(2)}) %collective-permute-start.5) | collective-permute-done | bytes 1048608 | tf_op jit(solution)/shard_map/cond/branch_2_fun/ppermute | solution.py:32
  375.4 17.2 %collective-permute-done.4 = bf16[256,2048]{1,0:T(8,128)(2,1)S(1)} collective-permute-done((bf16[256,2048]{1,0:T(8,128)(2,1)S(1)}, bf16[256,2048]{1,0:T(8,128)(2,1)S(1)}, u32[]{:S(2)}, u32[]{:S(2)}) %collective-permute-start.4) | collective-permute-done | bytes 1048608 | tf_op jit(solution)/shard_map/cond/branch_2_fun/ppermute | solution.py:32
  394.2 13.2 %fusion.34 = bf16[1024,2,128]{2,0,1:T(8,128)(2,1)} fusion(bf16[1024,2,128]{0,2,1:T(8,128)(2,1)S(1)} %copy-done.3, f32[2,1024,1024]{1,2,0:T(8,128)} %fusion.57, f32[2,1024,1024]{1,2,0:T(8,128)} %get-tuple-element.65, f32[2,1024]{1,0:T(2,128)S(1)} %get-tuple-element.64), kind=kOutput, calls=%fused_computation.32 | convolution fusion | flops 551816192 | bytes 17833984 | tf_op jit(solution)/shard_map/hqk,qhd->khd/dot_general | solution.py:75
  409.6 5.7 %all-to-all-start.5 = ((bf16[8,128,256]{1,2,0:T(8,128)(2,1)}), bf16[8,128,256]{1,2,0:T(8,128)(2,1)}, u32[]{:S(2)}, u32[]{:S(2)}) async-start(bf16[8,128,256]{1,2,0:T(8,128)(2,1)} %copy.83), calls=%async_computation.5 | async-start | bytes 1048576 | tf_op jit(solution)/shard_map/all_to_all | solution.py:135
  415.3 6.1 %add_multiply_fusion = (f32[256,2048]{1,0:T(8,128)}, f32[256,2048]{1,0:T(8,128)}) fusion(f32[256,2048]{1,0:T(8,128)} %get-tuple-element.62, f32[256,2048]{1,0:T(8,128)} %get-tuple-element.60, f32[256,2048]{1,0:T(8,128)S(1)} %get-tuple-element.61, f32[256,2048]{1,0:T(8,128)} %get-tuple-element.59), kind=kLoop, calls=%fused_computation.20 | loop fusion | flops 2097152 | bytes 12582912 | tf_op jit(solution)/shard_map/mul | solution.py:153
  421.4 2.0 copy.92
  424.5 2.0 copy.91
  (50 shorter events, 19.9 us)
Async XLA Ops:
  7.2 79.0 %copy-start = (bf16[128,2048]{1,0:T(8,128)(2,1)S(1)}, bf16[128,2048]{1,0:T(8,128)(2,1)}, u32[]{:S(2)}) copy-start(bf16[128,2048]{1,0:T(8,128)(2,1)} %param.16) | copy-start | bytes 1572868
  9.3 14.6 %all-to-all-start = ((bf16[128,8,256]{0,2,1:T(8,128)(2,1)}), bf16[128,8,256]{0,2,1:T(8,128)(2,1)S(1)}, u32[]{:S(2)}, u32[]{:S(2)}) async-start(bf16[128,8,256]{0,2,1:T(8,128)(2,1)} %bitcast.2), calls=%async_computation | async-start | bytes 1048576 | tf_op jit(solution)/shard_map/all_to_all | solution.py:125
  23.8 25.1 %all-to-all-start.1 = ((bf16[128,8,256]{0,2,1:T(8,128)(2,1)}), bf16[128,8,256]{0,2,1:T(8,128)(2,1)S(1)}, u32[]{:S(2)}, u32[]{:S(2)}) async-start(bf16[128,8,256]{0,2,1:T(8,128)(2,1)} %bitcast.4), calls=%async_computation.1 | async-start | bytes 1048576 | tf_op jit(solution)/shard_map/all_to_all | solution.py:126
  48.9 12.2 %all-to-all-start.3 = ((bf16[128,8,256]{0,2,1:T(8,128)(2,1)}), bf16[128,8,256]{0,2,1:T(8,128)(2,1)S(1)}, u32[]{:S(2)}, u32[]{:S(2)}) async-start(bf16[128,8,256]{0,2,1:T(8,128)(2,1)} %bitcast.8), calls=%async_computation.3 | async-start | bytes 1048576 | tf_op jit(solution)/shard_map/all_to_all | solution.py:127
  53.8 133.7 %reduce-scatter.2.cloned.1.call-start = ((), (), s32[]{:S(2)}) async-start(), calls=%async_computation.10 | async-start | bytes 9437184 | tf_op jit(solution)/shard_map/reduce_scatter | solution.py:139
  57.3 12.2 %copy-start.2 = (bf16[1024,2,128]{0,2,1:T(8,128)(2,1)}, bf16[1024,2,128]{0,2,1:T(8,128)(2,1)S(1)}, u32[]{:S(2)}) copy-start(bf16[1024,2,128]{0,2,1:T(8,128)(2,1)S(1)} %reshape.165) | copy-start | bytes 1572868
  57.9 11.6 %copy-start.4 = (bf16[1024,2,128]{0,2,1:T(8,128)(2,1)}, bf16[1024,2,128]{0,2,1:T(8,128)(2,1)S(1)}, u32[]{:S(2)}) copy-start(bf16[1024,2,128]{0,2,1:T(8,128)(2,1)S(1)} %reshape.166) | copy-start | bytes 1572868
  91.8 195.1 %all-gather.3.cloned.1.call-start = ((), (), s32[]{:S(2)}) async-start(), calls=%async_computation.9 | async-start | bytes 9437184 | tf_op jit(solution)/shard_map/all_gather | solution.py:117
  316.2 24.0 %all-to-all-start.6 = ((bf16[8,128,256]{1,2,0:T(8,128)(2,1)}), bf16[8,128,256]{1,2,0:T(8,128)(2,1)}, u32[]{:S(2)}, u32[]{:S(2)}) async-start(bf16[8,128,256]{1,2,0:T(8,128)(2,1)} %copy.85), calls=%async_computation.6 | async-start | bytes 1048576 | tf_op jit(solution)/shard_map/all_to_all | solution.py:136
  340.2 69.4 %all-to-all-start.4 = ((bf16[8,128,256]{1,2,0:T(8,128)(2,1)}), bf16[8,128,256]{1,2,0:T(8,128)(2,1)S(1)}, u32[]{:S(2)}, u32[]{:S(2)}) async-start(bf16[8,128,256]{1,2,0:T(8,128)(2,1)} %copy.80), calls=%async_computation.4 | async-start | bytes 1048576 | tf_op jit(solution)/shard_map/all_to_all | solution.py:134
  345.9 48.3 %copy-start.3 = (bf16[1024,2,128]{0,2,1:T(8,128)(2,1)S(1)}, bf16[1024,2,128]{0,2,1:T(8,128)(2,1)}, u32[]{:S(2)}) copy-start(bf16[1024,2,128]{0,2,1:T(8,128)(2,1)} %copy-done.2) | copy-start | bytes 1572868
  347.7 26.1 %collective-permute-start.5 = (bf16[256,2048]{1,0:T(8,128)(2,1)S(1)}, bf16[256,2048]{1,0:T(8,128)(2,1)S(1)}, u32[]{:S(2)}, u32[]{:S(2)}) collective-permute-start(bf16[256,2048]{1,0:T(8,128)(2,1)S(1)} %convert_element_type.92), channel_id=1, source_target_pairs={{0,32},{32,0},{8,40},{40,8},{16,48},{48,16},{24,56},{56,24},{64,96... | collective-permute-start | bytes 3145736 | tf_op jit(solution)/shard_map/cond/branch_2_fun/ppermute | solution.py:32
  349.5 43.1 %collective-permute-start.4 = (bf16[256,2048]{1,0:T(8,128)(2,1)S(1)}, bf16[256,2048]{1,0:T(8,128)(2,1)S(1)}, u32[]{:S(2)}, u32[]{:S(2)}) collective-permute-start(bf16[256,2048]{1,0:T(8,128)(2,1)S(1)} %convert_element_type.90), channel_id=1, source_target_pairs={{0,32},{32,0},{8,40},{40,8},{16,48},{48,16},{24,56},{56,24},{64,96... | collective-permute-start | bytes 3145736 | tf_op jit(solution)/shard_map/cond/branch_2_fun/ppermute | solution.py:32
  408.7 17.8 %copy-start.1 = (bf16[128,2048]{1,0:T(8,128)(2,1)S(1)}, bf16[128,2048]{1,0:T(8,128)(2,1)}, u32[]{:S(2)}) copy-start(bf16[128,2048]{1,0:T(8,128)(2,1)} %param.16) | copy-start | bytes 1572868
  409.6 14.8 %all-to-all-start.5 = ((bf16[8,128,256]{1,2,0:T(8,128)(2,1)}), bf16[8,128,256]{1,2,0:T(8,128)(2,1)}, u32[]{:S(2)}, u32[]{:S(2)}) async-start(bf16[8,128,256]{1,2,0:T(8,128)(2,1)} %copy.83), calls=%async_computation.5 | async-start | bytes 1048576 | tf_op jit(solution)/shard_map/all_to_all | solution.py:135
Sparse Core Ops, SparseCore 0:
  91.9 95.5 reduce-scatter.1
  193.6 93.2 all-gather.2
where the time goes:
time: 435 us; the launch traced here: 433 us
  waiting for transfers between devices  239 us (55%)
  matrix products  61 us (14%)
  blocking collectives  41.7 us (10%)
  starting transfers between devices  34.5 us (8%)
  local copies, waits for them, and re-layouts  21.9 us (5%)
  other arithmetic  20.3 us (5%)
  between operations  15 us (3%)
    reduce_scatter x1, waiting for transfers between devices, shards(): lax.psum_scatter(lax.dot_general(attended_tok, out_grad, (((0,), (0,)), (...  94.8 us
    all_gather x1, waiting for transfers between devices, shards(): lax.all_gather(weight16, 'fsdp', axis=0, tiled=True)  93.4 us
    ppermute x2, waiting for transfers between devices, swapped(): return lax.ppermute(block, axis, route)  41 us
    all_gather x1, blocking collectives, shards(): stem_ids = lax.all_gather(token_ids, 'fsdp', axis=0, tiled=True) // CODES  17.9 us
    dot_general x1, matrix products, head_attention(): jnp.einsum('hqk,qhd->khd', grad_score, query_h, preferred_element_type=jn...  13.2 us
    dot_general x1, matrix products, head_attention(): jnp.einsum('hqk,khd->qhd', grad_score, key_h, preferred_element_type=jnp....  12.8 us
    all_to_all x1, blocking collectives, shards(): lax.all_to_all(grad_tok, 'fsdp', split_axis=1, concat_axis=0, tiled=True)  12.6 us
    unnamed x20, local copies, waits for them, and re-layouts  11.7 us
  transfers between devices with their start and end apart: 10, of which 6 were waited for; matrix products, arithmetic and copies ran while one was open for 13% of the time, Pallas kernels for 0%

commit v1 on v0

v1 whole, which is shorter than its diff:
```python
import functools
import math

import jax
import jax.numpy as jnp
from jax import lax
from jax.experimental import pallas as pl
from jax.experimental.pallas import tpu as pltpu
from jax.sharding import PartitionSpec as P

HD = 128
INNER = 2048
MOMENTUM_RATE = 0.9
LEARN_RATE = 0.25
MESH = pl.DeviceIdType.MESH
NEG = -1e30
BF = jnp.bfloat16
F32 = jnp.float32
CT_MINOR = (((1,), (1,)), ((), ()))
CT_MAJOR = (((0,), (0,)), ((), ()))
CT_PLAIN = (((1,), (0,)), ((), ()))


def dot(a, b, dims):
    return lax.dot_general(a, b, dims, preferred_element_type=F32)


def kernel(
    bit, top,
    bm, q, k, v, og, params, mom, ids,
    dq, dk, dv, mo, pr, mr,
    qb, kb, vb, ogb, pf, mf, w16, m16, idb, skc, bias, pt, att, gr, dqb, dkb, dvb, dka, dva,
    ag_s, ag_r, a2a_s, a2a_r, id_s, id_r, bk_s, bk_r, px_s, px_r, loc,
):
    f = lax.axis_index("fsdp")
    d = lax.axis_index("dp")
    x = f // 4
    y = lax.rem(f, 4)

    def member(r):
        return lax.rem(x + r // 4, 2) * 4 + lax.rem(y + r % 4, 4)

    def back(r):
        return lax.rem(x + r // 4, 2) * 4 + lax.rem(y + 4 - r % 4, 4)

    width = 1 << bit
    partner = d + width - 2 * width * lax.rem(d // width, 2)
    to_partner = {"dp": partner}

    def rows(block, start=0, size=128):
        return pl.ds(pl.multiple_of(block * 128 + start, 16), size)

    def remote(src, dst, s_sem, r_sem, device):
        return pltpu.make_async_remote_copy(
            src_ref=src, dst_ref=dst, send_sem=s_sem, recv_sem=r_sem, device_id=device, device_id_type=MESH
        )

    own_rows = rows(f)
    locals_in = [
        pltpu.make_async_copy(params, pf, loc.at[0]),
        pltpu.make_async_copy(mom, mf, loc.at[1]),
        pltpu.make_async_copy(ids, idb.at[f], loc.at[2]),
    ]
    own_cols = pl.ds(pl.multiple_of(f * 256, 256), 256)
    for n, (src, dst) in enumerate(((q, qb), (k, kb), (v, vb))):
        locals_in.append(pltpu.make_async_copy(src.at[:, own_cols], dst.at[own_rows, :], loc.at[3 + n]))
    locals_in.append(pltpu.make_async_copy(og, ogb.at[own_rows, :], loc.at[6]))
    for copy in locals_in:
        copy.start()

    barrier = pltpu.get_barrier_semaphore()
    for r in range(1, 8):
        pl.semaphore_signal(barrier, inc=1, device_id={"fsdp": member(r)}, device_id_type=MESH)
    pl.semaphore_signal(barrier, inc=1, device_id=to_partner, device_id_type=MESH)
    pl.semaphore_wait(barrier, 8)

    n_x = {"fsdp": member(4)}
    y_p = {"fsdp": member(1)}
    y_m = {"fsdp": member(3)}
    sent = []

    def gather_send(n, block, start, size, device):
        part = ogb.at[rows(block, start, size), :]
        src = og if n < 3 else part
        copy = remote(src, part, ag_s.at[n], ag_r.at[n], device)
        copy.start()
        sent.append(copy)

    def gather_wait(n, block, start, size):
        part = ogb.at[rows(block, start, size), :]
        remote(part, part, ag_s.at[n], ag_r.at[n], n_x).wait_recv()

    for r in range(1, 8):
        copy = remote(ids, idb.at[f], id_s.at[r], id_r.at[r], {"fsdp": member(r)})
        copy.start()
        sent.append(copy)
    gather_send(0, f, 0, 128, n_x)
    gather_send(1, f, 0, 128, y_p)
    gather_send(2, f, 0, 128, y_m)

    for n, (src, dst) in enumerate(((q, qb), (k, kb), (v, vb))):
        for r in range(1, 8):
            g = member(r)
            cols = pl.ds(pl.multiple_of(g * 256, 256), 256)
            copy = remote(src.at[:, cols], dst.at[own_rows, :], a2a_s.at[n, r], a2a_r.at[n, r], {"fsdp": g})
            copy.start()
            sent.append(copy)

    locals_in[0].wait()

    def to_w16(n, _):
        part = pl.ds(pl.multiple_of(n * 32, 32), 32)
        w16[part, :] = pf[part, :].astype(BF)
        return 0

    lax.fori_loop(0, 8, to_w16, 0)
    locals_in[1].wait()
    locals_in[2].wait()
    for r in range(1, 8):
        remote(ids, idb.at[back(r)], id_s.at[r], id_r.at[r], n_x).wait_recv()

    def stem_col(g, _):
        stem = lax.shift_right_logical(idb[g], 11).astype(F32)
        spread = jnp.broadcast_to(stem, (128, 128))
        skc[pl.ds(pl.multiple_of(g * 128, 128), 128), :] = spread.T
        return 0

    lax.fori_loop(0, 8, stem_col, 0)
    swap_p = remote(w16, pr, px_s.at[0], px_r.at[0], to_partner)
    swap_p.start()

    iota_k = lax.broadcasted_iota(jnp.int32, (128, 128), 0)
    iota_q = lax.broadcasted_iota(jnp.int32, (128, 128), 1)
    tri = jnp.where(iota_k <= iota_q, 0.0, NEG).astype(F32)

    def bias_row(kg, _):
        k_rows = pl.ds(pl.multiple_of(kg * 128, 128), 128)
        sk = skc[k_rows, :]
        bias[k_rows, k_rows] = tri

        def bias_tile(qg, _):
            sq = lax.shift_right_logical(idb[qg], 11).astype(F32)
            sq = sq + (1 - bm[qg, kg]).astype(F32) * 16.0
            bias[k_rows, pl.ds(pl.multiple_of(qg * 128, 128), 128)] = jnp.where(sk == sq, 0.0, NEG)
            return 0

        lax.fori_loop(kg + 1, 8, bias_tile, 0)
        return 0

    lax.fori_loop(0, 8, bias_row, 0)
    for ip in range(4):
        bias[256 * ip + 128 : 256 * ip + 256, 256 * ip : 256 * ip + 128] = jnp.full((128, 128), NEG, F32)

    inv_width = 1.0 / math.sqrt(INNER)
    scale = 1.0 / math.sqrt(HD)
    scale2 = scale * math.log2(math.e)

    def grad_block(block):
        at = rows(block)
        gr[at, :] = (dot(ogb[at, :], w16[...], CT_MINOR) * inv_width).astype(BF)

    locals_in[6].wait()
    grad_block(f)

    gather_wait(0, member(4), 0, 128)
    gather_wait(1, member(3), 0, 128)
    gather_wait(2, member(1), 0, 128)
    gather_send(3, member(1), 0, 64, y_m)
    gather_send(4, member(3), 64, 64, y_p)
    gather_send(5, member(4), 0, top, y_p)
    gather_send(6, member(4), 0, top, y_m)
    if top < 128:
        gather_send(7, member(1), top, 128 - top, n_x)
        gather_send(8, member(3), top, 128 - top, n_x)
    grad_block(member(4))
    grad_block(member(1))
    grad_block(member(3))

    for n, (src, dst) in enumerate(((q, qb), (k, kb), (v, vb))):
        locals_in[3 + n].wait()
        for r in range(1, 8):
            land = dst.at[rows(back(r)), :]
            remote(land, land, a2a_s.at[n, r], a2a_r.at[n, r], n_x).wait_recv()

    def forward(ip):
        size = 256 * (ip + 1)
        here = slice(256 * ip, 256 * ip + 256)

        def head(h, _):
            hs = pl.ds(pl.multiple_of(h * 128, 128), 128)
            s = dot(kb[0:size, hs], qb[here, hs], CT_MINOR) * scale2 + bias[0:size, here]
            e = jnp.exp2(s - jnp.max(s, axis=0, keepdims=True))
            p = (e * (1.0 / jnp.sum(e, axis=0, keepdims=True))).astype(BF)
            pt[h, 0:size, here] = p
            att[hs, here] = dot(vb[0:size, hs], p, CT_MAJOR).astype(BF)
            return 0

        lax.fori_loop(0, 2, head, 0)

    half = top // 2
    forward(0)
    forward(1)
    gather_wait(3, member(2), 0, 64)
    gather_wait(4, member(2), 64, 64)
    if top < 128:
        gather_send(9, member(2), top, 128 - top, n_x)
    gather_wait(5, member(7), 0, top)
    gather_send(10, member(7), half, top - half, y_p)
    gather_wait(6, member(5), 0, top)
    gather_send(11, member(5), 0, half, y_m)
    forward(2)
    forward(3)
    grad_block(member(2))
    if top < 128:
        gather_wait(7, member(5), top, 128 - top)
        gather_wait(8, member(7), top, 128 - top)
    grad_block(member(5))
    grad_block(member(7))
    gather_wait(10, member(6), half, top - half)
    gather_wait(11, member(6), 0, half)
    if top < 128:
        gather_wait(9, member(6), top, 128 - top)

    def weight_cols(n, _):
        cols = pl.ds(pl.multiple_of(n * 256, 256), 256)
        moment = MOMENTUM_RATE * mf[:, cols] + dot(att[...], ogb[:, cols], CT_PLAIN) * inv_width
        mf[:, cols] = moment
        m16[:, cols] = moment.astype(BF)
        return 0

    lax.fori_loop(0, 8, weight_cols, 0)
    grad_block(member(6))
    swap_m = remote(m16, mr, px_s.at[1], px_r.at[1], to_partner)
    swap_m.start()
    out_m = pltpu.make_async_copy(mf, mo, loc.at[7])
    out_m.start()

    def backward(ip):
        size = 256 * (ip + 1)
        here = slice(256 * ip, 256 * ip + 256)

        def head(h, _):
            hs = pl.ds(pl.multiple_of(h * 128, 128), 128)
            g = gr[here, hs]
            p16 = pt[h, 0:size, here]
            p = p16.astype(F32)
            dp = dot(vb[0:size, hs], g, CT_MINOR)
            row_dot = jnp.sum(p * dp, axis=0, keepdims=True)
            ds = (p * (dp - row_dot) * scale).astype(BF)
            dv_part = dot(p16, g, CT_PLAIN)
            dk_part = dot(ds, qb[here, hs], CT_PLAIN)
            if ip == 3:
                dva[0:size, hs] = dv_part
                dka[0:size, hs] = dk_part
            else:
                dva[0:size, hs] += dv_part
                dka[0:size, hs] += dk_part
            dqb[here, hs] = dot(ds, kb[0:size, hs], CT_MAJOR).astype(BF)
            return 0

        lax.fori_loop(0, 2, head, 0)

    for ip in (3, 2, 1, 0):
        backward(ip)

    def finish(n, _):
        part = pl.ds(pl.multiple_of(n * 128, 128), 128)
        dkb[part, :] = dka[part, :].astype(BF)
        dvb[part, :] = dva[part, :].astype(BF)
        return 0

    lax.fori_loop(0, 8, finish, 0)
    outs = []
    for n, (src, dst) in enumerate(((dqb, dq), (dkb, dk), (dvb, dv))):
        for r in range(1, 8):
            g = member(r)
            copy = remote(src.at[rows(g), :], dst.at[:, own_cols], bk_s.at[n, r], bk_r.at[n, r], {"fsdp": g})
            copy.start()
            sent.append(copy)
        copy = pltpu.make_async_copy(src.at[own_rows, :], dst.at[:, own_cols], loc.at[8 + n])
        copy.start()
        outs.append(copy)
    for copy in sent:
        copy.wait_send()
    for n, (src, dst) in enumerate(((dqb, dq), (dkb, dk), (dvb, dv))):
        for r in range(1, 8):
            cols = pl.ds(pl.multiple_of(back(r) * 256, 256), 256)
            remote(src.at[own_rows, :], dst.at[:, cols], bk_s.at[n, r], bk_r.at[n, r], n_x).wait_recv()
    for copy in outs:
        copy.wait()
    out_m.wait()
    swap_p.wait()
    swap_m.wait()


def fused(bit, bm, q, k, v, og, params, mom, ids):
    anyspace = pl.BlockSpec(memory_space=pl.ANY)
    tok = jax.ShapeDtypeStruct((128, INNER), BF)
    dma = pltpu.SemaphoreType.DMA
    heads = pltpu.VMEM((1024, 256), BF)
    return pl.pallas_call(
        functools.partial(kernel, bit, 128 if bit == 1 else 64),
        name=f"step_{bit}",
        out_shape=(
            tok, tok, tok,
            jax.ShapeDtypeStruct((256, INNER), F32),
            jax.ShapeDtypeStruct((256, INNER), BF),
            jax.ShapeDtypeStruct((256, INNER), BF),
        ),
        in_specs=[pl.BlockSpec(memory_space=pltpu.SMEM)] + [anyspace] * 7,
        out_specs=(anyspace,) * 6,
        scratch_shapes=[
            heads, heads, heads,
            pltpu.VMEM((1024, INNER), BF),
            pltpu.VMEM((256, INNER), F32),
            pltpu.VMEM((256, INNER), F32),
            pltpu.VMEM((256, INNER), BF),
            pltpu.VMEM((256, INNER), BF),
            pltpu.VMEM((8, 1, 128), jnp.int32),
            pltpu.VMEM((1024, 128), F32),
            pltpu.VMEM((1024, 1024), F32),
            pltpu.VMEM((2, 1024, 1024), BF),
            pltpu.VMEM((256, 1024), BF),
            heads, heads, heads, heads,
            pltpu.VMEM((1024, 256), F32),
            pltpu.VMEM((1024, 256), F32),
            dma((12,)), dma((12,)), dma((3, 8)), dma((3, 8)), dma((8,)), dma((8,)),
            dma((3, 8)), dma((3, 8)), dma((2,)), dma((2,)), dma((11,)),
        ],
        compiler_params=pltpu.CompilerParams(
            collective_id=bit, has_side_effects=True, vmem_limit_bytes=60 * 1024 * 1024
        ),
    )(bm, q, k, v, og, params, mom, ids)


def shards(q, k, v, og, params, mom, token_ids, block_mask, step_index):
    step_value = step_index[0]
    correction = 1.0 / (1.0 - jnp.exp((step_value + 1).astype(F32) * math.log(MOMENTUM_RATE)))
    rate = LEARN_RATE * correction
    ids = token_ids.reshape(1, 128)
    dq, dk, dv, moment, other_p, other_m = lax.switch(
        step_value % 4,
        [functools.partial(fused, bit) for bit in range(4)],
        block_mask, q, k, v, og, params, mom, ids,
    )
    other_m = other_m.astype(F32)
    new_params = 0.5 * ((params - rate * moment) + (other_p.astype(F32) - rate * other_m))
    new_momentum = 0.5 * (moment + other_m)
    return dq, dk, dv, new_params, new_momentum


def solution(mesh):
    split = P(("dp", "fsdp"), None)
    return jax.shard_map(
        shards,
        mesh=mesh,
        in_specs=(split,) * 6 + (P(("dp", "fsdp")), P(), P()),
        out_specs=(split,) * 5,
        check_vma=False,
    )
```

time: 435 us -> 113 us (0.26)
  waiting for transfers between devices: 239 us -> 0 us
  Pallas kernels: 0 us -> 104 us
  matrix products: 61 us -> 0 us
  blocking collectives: 41.7 us -> 0 us
  starting transfers between devices: 34.5 us -> 0 us
  local copies, waits for them, and re-layouts: 21.9 us -> 2.39 us
  other arithmetic: 20.3 us -> 4.76 us
  between operations: 15 us -> 1.4 us
    pallas_call x0 -> x1, Pallas kernels: none -> 104 us  [fused(): pl.pallas_call(functools.partial(kernel, bit, 128 if bit == 1 else 64), n...]
    reduce_scatter x1 -> x0, waiting for transfers between devices: 94.8 us -> none  [shards(): lax.psum_scatter(lax.dot_general(attended_tok, out_grad, (((0,), (0,)), (...]
    all_gather x1 -> x0, waiting for transfers between devices: 93.4 us -> none  [shards(): lax.all_gather(weight16, 'fsdp', axis=0, tiled=True)]
    dot_general x7 -> x0, matrix products: 53.2 us -> none  [the longest x1 13.2 us: head_attention(): jnp.einsum('hqk,qhd->khd', grad_score, query_h, preferred_element_type=jn...]
    ppermute x2 -> x0, waiting for transfers between devices: 41 us -> none  [swapped(): return lax.ppermute(block, axis, route)]
    all_to_all x6 -> x0, starting transfers between devices: 32.1 us -> none  [the longest x1 5.93 us: shards(): lax.all_to_all(query_rows, 'fsdp', split_axis=1, concat_axis=0, tiled=True)]
    all_to_all x2 -> x0, blocking collectives: 23.8 us -> none  [the longest x1 12.6 us: shards(): lax.all_to_all(grad_tok, 'fsdp', split_axis=1, concat_axis=0, tiled=True)]
    all_gather x1 -> x0, blocking collectives: 17.9 us -> none  [shards(): stem_ids = lax.all_gather(token_ids, 'fsdp', axis=0, tiled=True) // CODES]
  transfers between devices with their start and end apart: 10 -> 0, of which waited for: 6 -> 0; matrix products, arithmetic and copies ran while one was open for 13% -> 0% of each run, Pallas kernels for 0% -> 0%
where the time goes in v1:
time: 113 us
  Pallas kernels  104 us (92%)
  other arithmetic  4.76 us (4%)
  local copies, waits for them, and re-layouts  2.39 us (2%)
  between operations  1.4 us (1%)
    pallas_call x1, Pallas kernels, fused(): pl.pallas_call(functools.partial(kernel, bit, 128 if bit == 1 else 64), n...  104 us
    mul x1, other arithmetic, shards(): new_momentum = 0.5 * (moment + other_m)  4.76 us
    unnamed x7, local copies, waits for them, and re-layouts  2.39 us

profile of v1, /device:TPU:2, one launch (start us, length us, event | category | flops | bytes accessed | tf_op | source)
XLA Modules:
  0.0 113.0 jit_solution(1898706729907787629)
XLA Ops:
  1.4 104.5 %conditional.1 = ((bf16[128,2048]{1,0:T(8,128)(2,1)S(1)}, bf16[128,2048]{1,0:T(8,128)(2,1)}, bf16[128,2048]{1,0:T(8,128)(2,1)}, f32[256,2048]{1,0:T(8,128)S(1)},...) conditional(s32[]{:T(128)} %clamp.3, (s32[8,8]{1,0:T(8,128)}, ...), branch_computations={%region_0.1_spmd, %region_1.2_spmd, %region_2.3_spmd, %region_3.4_... | conditional | bytes 8 | solution.py:341
  1.6 103.7 %step_1.1 = (bf16[128,2048]{1,0:T(8,128)(2,1)S(1)}, bf16[128,2048]{1,0:T(8,128)(2,1)}, bf16[128,2048]{1,0:T(8,128)(2,1)}, f32[256,2048]{1,0:T(8,128)S(1)}, bf16[...) custom-call(s32[8,8]{1,0:T(8,128)} %get-tuple-element.105.bm, bf16[128,2048]{1,0:T(8,128)(2,1)} %get-tuple-element.106.q, ...), custom_call_target="tpu_custom_call" | custom-call | tf_op jit(solution)/shard_map/cond/branch_1_fun/step_1/pallas_call | solution.py:301
  105.8 0.0 copy-start
  105.9 4.8 %fusion = (f32[256,2048]{1,0:T(8,128)}, f32[256,2048]{1,0:T(8,128)}) fusion(f32[256,2048]{1,0:T(8,128)S(1)} %get-tuple-element.175, bf16[256,2048]{1,0:T(8,128)(2,1)} %get-tuple-element.173, bf16[256,2048]{1,0:T(8,128)(2,1)S(1)} %get-tuple-element.174, f32[256,2048]{1,0:T(8,128)} %param.17, f32[]{:T(128)S(6)} %mul_shard_map.3), kind=kLoop, calls=%fused_computation.2 | loop fusion | flops 5242880 | bytes 10485764 | tf_op jit(solution)/shard_map/mul | solution.py:348
  110.6 0.0 copy-start.1
  110.6 0.8 copy.42
  111.4 0.0 copy-done
  111.4 0.8 copy.43
  112.2 0.0 copy-done.1
  112.2 0.8 copy.44
Async XLA Ops:
  105.8 5.6 %copy-start = (bf16[128,2048]{1,0:T(8,128)(2,1)S(1)}, bf16[128,2048]{1,0:T(8,128)(2,1)}, u32[]{:S(2)}) copy-start(bf16[128,2048]{1,0:T(8,128)(2,1)} %get-tuple-element.215) | copy-start | bytes 1572868
  110.6 1.6 %copy-start.1 = (bf16[128,2048]{1,0:T(8,128)(2,1)S(1)}, bf16[128,2048]{1,0:T(8,128)(2,1)}, u32[]{:S(2)}) copy-start(bf16[128,2048]{1,0:T(8,128)(2,1)} %get-tuple-element.216) | copy-start | bytes 1572868
